TPU v7x, 256 devices: a whole 4x4x8 slice. The times are simulated.
256 devices in a mesh: seq: 64 (over z, x, core), head: 4 (over y).
Axes of the slice: x: 4, y: 4, z: 8, core: 2. Of those that a mesh axis runs over, the one named last changes fastest.
Arguments:
- queries: bfloat16 [32768, 4096], P(('seq', 'head')), may hold values from -6 to 6
- keys: bfloat16 [32768, 4096], P(('seq', 'head')), may hold values from -6 to 6
- values: bfloat16 [32768, 4096], P(('seq', 'head')), may hold values from -128 to 128
- out_grad: bfloat16 [32768, 4096], P(('seq', 'head')), may hold values from -16 to 16
- doc_lengths: int32 [8], replicated, may hold values from 1 to 16384, 32768 in all
Outputs:
- attn_out: bfloat16 [32768, 4096], P(('seq', 'head'))
- grad_queries: bfloat16 [32768, 4096], P(('seq', 'head'))
- grad_keys: bfloat16 [32768, 4096], P(('seq', 'head'))
- grad_values: bfloat16 [32768, 4096], P(('seq', 'head'))
Inputs may be any that keep to these rules, and one draw needn't show every extreme that they name: `doc_lengths`: the lengths sum to 32768; the longest is exactly 16384.
All inputs are finite; a program needn't handle non-finite values.
Results may differ from a plain program's by a relative error of at most 0.011.
Values may be sent and summed in bfloat16 or wider, within the bound.
A program may use at most 128 MiB of HBM per device.

v0:
```python
import jax
import jax.numpy as jnp
from jax import lax
from jax.sharding import PartitionSpec as P

DH = 128


def prefix(value, axis, join, neutral):
    count, mine = (lax.axis_size(axis), lax.axis_index(axis))
    pieces = jax.tree.map(lambda part: lax.all_gather(part, axis), value)
    so_far = jax.tree.map(
        lambda part, zero: jnp.full_like(part, 0) + jnp.asarray(zero, part.dtype), value, neutral
    )

    def lap(position, so_far):
        longer = join(so_far, jax.tree.map(lambda part: part[position], pieces))
        return jax.tree.map(lambda new, old: jnp.where(position < mine, new, old), longer, so_far)

    return lax.fori_loop(0, count - 1, lap, so_far)


def prefix_2(array, axis, join, neutral):
    count = lax.axis_size(axis)
    place = lax.axis_index(axis)
    ahead = count - 1 - place
    gathered = jax.tree.map(
        lambda a, kind: lax.all_gather(a.astype(kind), axis), array, (jnp.bfloat16, jnp.bfloat16)
    )
    state = jax.tree.map(lambda a, e: jnp.zeros_like(a) + jnp.asarray(e, a.dtype), array, neutral)

    def one(lap, state):
        source = count - 1 - lap
        return join(
            state,
            jax.tree.map(
                lambda a, own: lax.dynamic_index_in_dim(a, source, 0, False).astype(own.dtype),
                gathered,
                array,
            ),
        )

    return lax.fori_loop(0, ahead, one, state)


def feature(array):
    wide = array.astype(jnp.float32)
    return jnp.where(wide > 0, wide + 1.0, jnp.exp(jnp.minimum(wide, 0.0)))


def slope(array):
    wide = array.astype(jnp.float32)
    return jnp.where(wide > 0, 1.0, jnp.exp(jnp.minimum(wide, 0.0)))


def doc_index(doc_ends, where):
    return jnp.sum((jnp.asarray(where)[..., None] >= doc_ends).astype(jnp.int32), axis=-1)


def linked(earlier, later):
    return (later[0] + (1.0 - later[1]) * earlier[0], jnp.maximum(earlier[1], later[1]))


def local(queries, keys, values, out_grad, doc_lengths):
    shared = (
        lax.all_to_all(queries, "head", split_axis=1, concat_axis=0, tiled=True),
        lax.all_to_all(keys, "head", split_axis=1, concat_axis=0, tiled=True),
        lax.all_to_all(values, "head", split_axis=1, concat_axis=0, tiled=True),
        lax.all_to_all(out_grad, "head", split_axis=1, concat_axis=0, tiled=True),
    )
    block_len = shared[0].shape[0]
    head_count = shared[0].shape[1] // DH
    query_rows = shared[0].reshape(block_len, head_count, DH)
    key_rows = shared[1].reshape(block_len, head_count, DH)
    value_rows = shared[2].reshape(block_len, head_count, DH)
    grad_rows = shared[3].reshape(block_len, head_count, DH)
    block_index = lax.axis_index("seq")
    doc_ends = jnp.cumsum(doc_lengths)
    block_start = block_index * block_len
    within = jnp.arange(block_len, dtype=jnp.int32)
    doc_of = doc_index(doc_ends, block_start + within)
    doc_first = doc_of[0]
    doc_last = doc_of[block_len - 1]
    before = doc_index(doc_ends, block_start - 1)
    doc_after = doc_index(doc_ends, block_start + block_len)
    visible = (within[:, None] >= within[None, :]) & (doc_of[:, None] == doc_of[None, :])
    head_rows = (doc_of == doc_first)[:, None, None]
    tail_rows = (doc_of == doc_last)[:, None, None]
    tile_rows = 256
    tile_count = block_len // tile_rows
    feat_query = feature(query_rows).astype(jnp.bfloat16)
    feat_key = feature(key_rows).astype(jnp.bfloat16)
    zero_bf = jnp.zeros((), jnp.bfloat16)
    tail_state = jnp.einsum(
        "shd,she->hde",
        jnp.where(tail_rows, feat_key, zero_bf),
        value_rows,
        preferred_element_type=jnp.float32,
    )
    reset_flag = (doc_last != before).astype(jnp.float32)
    carried, _ = prefix(
        (tail_state, reset_flag),
        "seq",
        linked,
        (jnp.zeros_like(tail_state), jnp.zeros((), jnp.float32)),
    )
    incoming = jnp.where(doc_first == before, carried, 0.0).astype(jnp.bfloat16)
    score_tiles = []
    normed_tiles = []
    grad_att_tiles = []
    for tile in range(tile_count):
        first = tile * tile_rows
        last = first + tile_rows
        query_tile = feat_query[first:last]
        tile_scores = jnp.einsum(
            "thd,shd->hts", query_tile, feat_key[:last], preferred_element_type=jnp.float32
        )
        tile_scores = jnp.where(visible[first:last, :last][None], tile_scores, 0.0).astype(
            jnp.bfloat16
        )
        attended = jnp.einsum(
            "hts,she->the", tile_scores, value_rows[:last], preferred_element_type=jnp.float32
        )
        attended = attended + jnp.where(
            head_rows[first:last],
            jnp.einsum("thd,hde->the", query_tile, incoming, preferred_element_type=jnp.float32),
            0.0,
        )
        inv_rms = lax.rsqrt(jnp.mean(attended * attended, axis=-1, keepdims=True) + 1e-05)
        normed = attended * inv_rms
        grad_out = grad_rows[first:last].astype(jnp.float32)
        grad_att_tile = (
            (grad_out - normed * jnp.mean(grad_out * normed, axis=-1, keepdims=True)) * inv_rms
        ).astype(jnp.bfloat16)
        score_tiles.append(tile_scores)
        normed_tiles.append(normed.astype(jnp.bfloat16))
        grad_att_tiles.append(grad_att_tile)
    out_block = jnp.concatenate(normed_tiles, axis=0).reshape(block_len, head_count * DH)
    grad_att = jnp.concatenate(grad_att_tiles, axis=0)
    attn_out = lax.all_to_all(out_block, "head", split_axis=0, concat_axis=1, tiled=True)
    head_sum = jnp.einsum(
        "thd,the->hde",
        jnp.where(head_rows, feat_query, zero_bf),
        grad_att,
        preferred_element_type=jnp.float32,
    )
    reset_back = (doc_first != doc_after).astype(jnp.float32)
    future, _ = prefix_2(
        (head_sum, reset_back),
        "seq",
        linked,
        (jnp.zeros_like(head_sum), jnp.zeros((), jnp.float32)),
    )
    outgoing = jnp.where(doc_last == doc_after, future, 0.0).astype(jnp.bfloat16)
    grad_fk = jnp.zeros((block_len, head_count, DH), jnp.float32)
    grad_fv = jnp.zeros((block_len, head_count, DH), jnp.float32)
    grad_fq_tiles = []
    for tile in range(tile_count):
        first = tile * tile_rows
        last = first + tile_rows
        grad_tile = grad_att_tiles[tile]
        tile_grads = jnp.einsum(
            "the,she->hts", grad_tile, value_rows[:last], preferred_element_type=jnp.float32
        )
        tile_grads = jnp.where(visible[first:last, :last][None], tile_grads, 0.0).astype(
            jnp.bfloat16
        )
        grad_fq_tile = jnp.einsum(
            "hts,shd->thd", tile_grads, feat_key[:last], preferred_element_type=jnp.float32
        )
        grad_fq_tile = grad_fq_tile + jnp.where(
            head_rows[first:last],
            jnp.einsum("the,hde->thd", grad_tile, incoming, preferred_element_type=jnp.float32),
            0.0,
        )
        grad_fq_tiles.append(grad_fq_tile)
        grad_fk = grad_fk.at[:last].add(
            jnp.einsum(
                "hts,thd->shd",
                tile_grads,
                feat_query[first:last],
                preferred_element_type=jnp.float32,
            )
        )
        grad_fv = grad_fv.at[:last].add(
            jnp.einsum(
                "hts,the->she", score_tiles[tile], grad_tile, preferred_element_type=jnp.float32
            )
        )
    grad_fq = jnp.concatenate(grad_fq_tiles, axis=0)
    grad_fk = grad_fk + jnp.where(
        tail_rows,
        jnp.einsum("she,hde->shd", value_rows, outgoing, preferred_element_type=jnp.float32),
        0.0,
    )
    grad_fv = grad_fv + jnp.where(
        tail_rows,
        jnp.einsum("shd,hde->she", feat_key, outgoing, preferred_element_type=jnp.float32),
        0.0,
    )
    grad_query = (
        (grad_fq * slope(query_rows)).astype(jnp.bfloat16).reshape(block_len, head_count * DH)
    )
    grad_key = (grad_fk * slope(key_rows)).astype(jnp.bfloat16).reshape(block_len, head_count * DH)
    grad_value = grad_fv.astype(jnp.bfloat16).reshape(block_len, head_count * DH)
    grad_queries, grad_keys, grad_values = (
        lax.all_to_all(grad_query, "head", split_axis=0, concat_axis=1, tiled=True),
        lax.all_to_all(grad_key, "head", split_axis=0, concat_axis=1, tiled=True),
        lax.all_to_all(grad_value, "head", split_axis=0, concat_axis=1, tiled=True),
    )
    return (attn_out, grad_queries, grad_keys, grad_values)


def solution(mesh):
    placed = (
        P(("seq", "head"), None),
        P(("seq", "head"), None),
        P(("seq", "head"), None),
        P(("seq", "head"), None),
        P(),
    )
    return jax.shard_map(
        local,
        mesh=mesh,
        in_specs=placed,
        out_specs=(
            P(("seq", "head"), None),
            P(("seq", "head"), None),
            P(("seq", "head"), None),
            P(("seq", "head"), None),
        ),
        check_vma=False,
    )
```

profile of v0, /device:TPU:8, one launch (start us, length us, event | category | flops | bytes accessed | tf_op | source)
XLA Modules:
  0.0 783.8 jit_solution(12176665650693809135)
XLA Ops:
  7.2 2.4 copy.285
  9.5 5.8 all-to-all-start.1
  16.6 11.7 %all-to-all-done.1 = bf16[128,4,1024]{2,0,1:T(8,128)(2,1)S(1)} async-done(((bf16[128,4,1024]{2,0,1:T(8,128)(2,1)}), bf16[128,4,1024]{2,0,1:T(8,128)(2,1)S(1)}, u32[]{:S(2)}, u32[]{:S(2)}) %all-to-all-start.1) | async-done | bytes 1048608 | tf_op jit(solution)/shard_map/all_to_all | solution.py:67
  28.2 4.9 all-to-all-start.2
  37.7 7.5 all-to-all-done.2
  49.8 5.8 all-to-all-start
  59.1 2.3 copy.283
  62.7 134.0 %all-reduce.2 = f32[64]{0:T(128)S(1)} all-reduce(f32[64]{0:T(128)S(1)} %dynamic-update-slice.10), channel_id=1, replica_groups=mesh['seq'=64,'head'=4] {'seq'}, use_global_device_ids=true, to_apply=%add.2 | all-reduce | flops 64 | bytes 512
  196.8 4.7 all-to-all-start.4
  201.5 2.7 fusion.2
  213.7 2.5 slice_convert_fusion.1
  220.3 2.5 copy.250
  223.1 2.8 bitcast_select_fusion
  232.7 168.2 %while.35 = (s32[]{:T(128)}, f32[8,128,128]{2,1,0:T(8,128)S(1)}, s32[]{:T(128)}, f32[64,8,128,128]{3,2,1,0:T(8,128)}, f32[64]{0:T(128)S(1)}, /*index=5*/s32[]{:T(128)}, f32[1]{0:T(128)}, s32[]{:T(128)}) while((s32[]{:T(128)}, f32[8,128,128]{2,1,0:T(8,128)S(1)}, s32[]{:T(128)}, f32[64,8,128,128]{3,2,1,0:T(8,128)}, f32[64]{0:T(128)S(1)}, ...), condition=%wide.region_4.5_spmd.clone, body=%wide.region_3.4_spmd.clone.sunk | while | flops 524293 | bytes 1573001 | solution.py:20
  412.2 2.5 copy.201
  418.2 2.6 copy.208
  420.8 2.9 pad_maximum_fusion
  423.7 2.9 copy.236
  426.6 3.4 fusion.7
  430.0 5.4 all-to-all-start.5
  438.7 126.2 %all-reduce.3 = bf16[64]{0:T(256)(128)(2,1)S(1)} all-reduce(bf16[64]{0:T(256)(128)(2,1)S(1)} %dynamic-update-slice.11), channel_id=1, replica_groups=mesh['seq'=64,'head'=4] {'seq'}, use_global_device_ids=true, to_apply=%add.3 | all-reduce | flops 64 | bytes 256
  564.9 3.4 copy.252
  568.3 3.0 copy.237
  573.0 2.3 all_to_all.105
  575.4 2.5 convolution_bitcast_fusion.1
  579.8 4.8 all-to-all-start.3
  584.6 153.4 %while.34 = (s32[]{:T(128)}, f32[8,128,128]{2,1,0:T(8,128)S(1)}, s32[]{:T(128)}, bf16[64,8,128,128]{3,2,1,0:T(8,128)(2,1)}, bf16[64]{0:T(256)(128)(2,1)S(1)}, /*...) while((s32[]{:T(128)}, f32[8,128,128]{2,1,0:T(8,128)S(1)}, s32[]{:T(128)}, ...), condition=%wide.region_11.12_spmd, body=%wide.region_10.11_spmd.sunk | while | flops 393223 | bytes 1310893 | solution.py:43
  738.0 3.4 fusion.12
  743.5 2.4 copy.221
  745.9 4.9 all-to-all-start.7
  756.4 4.9 all-to-all-done.7
  761.2 4.9 all-to-all-start.6
  (404 shorter events, 311.2 us)
Async XLA Ops:
  7.2 8.2 %copy-start.29 = (bf16[128,4096]{1,0:T(8,128)(2,1)S(1)}, bf16[128,4096]{1,0:T(8,128)(2,1)}, u32[]{:S(2)}) copy-start(bf16[128,4096]{1,0:T(8,128)(2,1)} %param.23) | copy-start | bytes 3145732
  9.5 6.8 copy-start.33
  9.5 18.7 %all-to-all-start.1 = ((bf16[128,4,1024]{2,0,1:T(8,128)(2,1)}), bf16[128,4,1024]{2,0,1:T(8,128)(2,1)S(1)}, u32[]{:S(2)}, u32[]{:S(2)}) async-start(bf16[128,4,1024]{2,0,1:T(8,128)(2,1)} %bitcast.161), calls=%async_computation.1 | async-start | bytes 2097152 | tf_op jit(solution)/shard_map/all_to_all | solution.py:67
  28.2 17.0 %all-to-all-start.2 = ((bf16[128,4,1024]{2,0,1:T(8,128)(2,1)}), bf16[128,4,1024]{2,0,1:T(8,128)(2,1)S(1)}, u32[]{:S(2)}, u32[]{:S(2)}) async-start(bf16[128,4,1024]{2,0,1:T(8,128)(2,1)} %bitcast.160), calls=%async_computation.2 | async-start | bytes 2097152 | tf_op jit(solution)/shard_map/all_to_all | solution.py:68
  33.2 199.6 %all-gather.5.cloned.1.call-start = ((), (), s32[]{:S(2)}) async-start(), calls=%async_computation.8 | async-start | bytes 34078720 | tf_op jit(solution)/shard_map/all_gather | solution.py:11
  49.8 11.7 %copy-start.34 = (u32[256]{0:T(256)S(1)}, u32[256]{0:T(256)}, u32[]{:S(2)}) copy-start(u32[256]{0:T(256)} %constant.223) | copy-start | bytes 3076
  49.8 146.9 %all-to-all-start = ((bf16[128,4,1024]{2,0,1:T(8,128)(2,1)}), bf16[128,4,1024]{2,0,1:T(8,128)(2,1)}, u32[]{:S(2)}, u32[]{:S(2)}) async-start(bf16[128,4,1024]{2,0,1:T(8,128)(2,1)} %bitcast.162), calls=%async_computation | async-start | bytes 2097152 | tf_op jit(solution)/shard_map/all_to_all | solution.py:66
  59.1 169.7 %copy-start.31 = (pred[256,512]{1,0:T(8,128)(4,1)}, pred[256,512]{1,0:T(8,128)(4,1)S(1)}, u32[]{:S(2)}) copy-start(pred[256,512]{1,0:T(8,128)(4,1)S(1)} %slice.160) | copy-start | bytes 393220
  196.8 16.9 %all-to-all-start.4 = ((bf16[128,4,1024]{2,0,1:T(8,128)(2,1)}), bf16[128,4,1024]{2,0,1:T(8,128)(2,1)}, u32[]{:S(2)}, u32[]{:S(2)}) async-start(bf16[128,4,1024]{2,0,1:T(8,128)(2,1)} %bitcast.191), calls=%async_computation.4 | async-start | bytes 2097152 | tf_op jit(solution)/shard_map/all_to_all | solution.py:69
  201.5 383.1 %all-gather.7.cloned.1.call-start = ((), (), s32[]{:S(2)}) async-start(), calls=%async_computation.9 | async-start | bytes 17039360 | tf_op jit(solution)/shard_map/all_gather | solution.py:28
  207.3 193.7 %copy-start.4 = (bf16[256,8,128]{0,2,1:T(8,128)(2,1)}, bf16[256,8,128]{0,2,1:T(8,128)(2,1)S(1)}, u32[]{:S(2)}) copy-start(bf16[256,8,128]{0,2,1:T(8,128)(2,1)S(1)} %copy.211) | copy-start | bytes 1572868
  213.7 3.6 copy-start.27
  222.8 3.1 copy-start.18
  223.1 4.3 copy-start.24
  225.9 2.9 copy-start.12
  401.0 2.7 copy-start.13
  401.1 2.7 copy-start.22
  407.2 3.3 copy-start.17
  407.2 9.1 %copy-start.15 = (bf16[256,8,128]{2,0,1:T(8,128)(2,1)}, bf16[256,8,128]{2,0,1:T(8,128)(2,1)S(1)}, u32[]{:S(2)}) copy-start(bf16[256,8,128]{2,0,1:T(8,128)(2,1)S(1)} %get-tuple-element.302) | copy-start | bytes 1572868
  410.9 3.8 copy-start.32
  418.2 2.6 copy-start.23
  430.0 149.8 %all-to-all-start.5 = ((bf16[4,128,1024]{2,1,0:T(8,128)(2,1)}), bf16[4,128,1024]{2,1,0:T(8,128)(2,1)}, u32[]{:S(2)}, u32[]{:S(2)}) async-start(bf16[4,128,1024]{2,1,0:T(8,128)(2,1)} %fusion.7), calls=%async_computation.5 | async-start | bytes 2097152 | tf_op jit(solution)/shard_map/all_to_all | solution.py:207
  568.3 3.0 copy-start.25
  568.3 3.0 copy-start.26
  571.4 4.0 copy-start.1
  575.3 2.5 copy-start.7
  575.3 2.5 copy-start.16
  579.8 166.1 %all-to-all-start.3 = ((bf16[4,128,1024]{2,1,0:T(8,128)(2,1)}), bf16[4,128,1024]{2,1,0:T(8,128)(2,1)}, u32[]{:S(2)}, u32[]{:S(2)}) async-start(bf16[4,128,1024]{2,1,0:T(8,128)(2,1)} %all_to_all.105), calls=%async_computation.3 | async-start | bytes 2097152 | tf_op jit(solution)/shard_map/all_to_all | solution.py:140
  743.5 7.3 copy-start.5
  745.9 6.6 copy-start.14
  745.9 15.4 %all-to-all-start.7 = ((bf16[4,128,1024]{1,2,0:T(8,128)(2,1)}), bf16[4,128,1024]{1,2,0:T(8,128)(2,1)}, u32[]{:S(2)}, u32[]{:S(2)}) async-start(bf16[4,128,1024]{1,2,0:T(8,128)(2,1)} %copy.221), calls=%async_computation.7 | async-start | bytes 2097152 | tf_op jit(solution)/shard_map/all_to_all | solution.py:209
  761.2 14.4 %all-to-all-start.6 = ((bf16[4,128,1024]{1,2,0:T(8,128)(2,1)}), bf16[4,128,1024]{1,2,0:T(8,128)(2,1)S(1)}, u32[]{:S(2)}, u32[]{:S(2)}) async-start(bf16[4,128,1024]{1,2,0:T(8,128)(2,1)} %copy.216), calls=%async_computation.6 | async-start | bytes 2097152 | tf_op jit(solution)/shard_map/all_to_all | solution.py:208
  (13 other events, 21.2 us)
Sparse Core Ops, SparseCore 0:
  48.9 145.0 all-gather.4
  408.5 95.4 all-gather.6
where the time goes:
time: 791 us; the launch traced here: 784 us
  blocking collectives  260 us (33%)
  other arithmetic  191 us (24%)
  local copies, waits for them, and re-layouts  139 us (18%)
  loops' own time  80.8 us (10%)
  starting transfers between devices  41.4 us (5%)
  matrix products  26.3 us (3%)
  waiting for transfers between devices  26 us (3%)
  between operations  19.7 us (2%)
    unnamed x2, blocking collectives  260 us
    select_n x63, other arithmetic, lap(): jnp.where(position < mine, new, old)  93.2 us
    add x63, other arithmetic, linked(): later[0] + (1.0 - later[1]) * earlier[0]  73.2 us
    another operation x1, loops' own time, prefix_2(): return lax.fori_loop(0, ahead, one, state)  43 us
    another operation x1, loops' own time, prefix(): return lax.fori_loop(0, count - 1, lap, so_far)  37.8 us
    dynamic_slice x63, local copies, waits for them, and re-layouts, lap(): longer = join(so_far, jax.tree.map(lambda part: part[position], pieces))  37.2 us
    dynamic_slice x63, local copies, waits for them, and re-layouts, one(): lax.dynamic_index_in_dim(a, source, 0, False).astype(own.dtype)  37.2 us
    unnamed x88, local copies, waits for them, and re-layouts  23.2 us
  transfers between devices with their start and end apart: 10, of which 4 were waited for; matrix products, arithmetic and copies ran while one was open for 26% of the time, Pallas kernels for 0%

commit v1 on v0

--- a/solution.py
+++ b/solution.py
@@ -64,7 +64,10 @@
 def local(queries, keys, values, out_grad, doc_lengths):
     shared = (
         lax.all_to_all(queries, "head", split_axis=1, concat_axis=0, tiled=True),
-        lax.all_to_all(keys, "head", split_axis=1, concat_axis=0, tiled=True),
+        jnp.concatenate(
+            lax.all_to_all(jnp.stack(jnp.split(keys, lax.axis_size("head"), axis=1)), "head", 0, 0),
+            axis=0,
+        ),
         lax.all_to_all(values, "head", split_axis=1, concat_axis=0, tiled=True),
         lax.all_to_all(out_grad, "head", split_axis=1, concat_axis=0, tiled=True),
     )

time: 791 us -> 813 us (1.028)
  waiting for transfers between devices: 26 us -> 35.8 us
  local copies, waits for them, and re-layouts: 139 us -> 148 us
    all_to_all x1, waiting for transfers between devices: 0.01 us -> 8.39 us  [local(): lax.all_to_all(queries, 'head', split_axis=1, concat_axis=0, tiled=True)]
    unnamed x88 -> x94, local copies, waits for them, and re-layouts: 23.2 us -> 24.4 us
  transfers between devices with their start and end apart: 10 -> 10, of which waited for: 4 -> 5; matrix products, arithmetic and copies ran while one was open for 26% -> 26% of each run, Pallas kernels for 0% -> 0%
where the time goes in v1:
time: 813 us; the launch traced here: 806 us
  blocking collectives  260 us (32%)
  other arithmetic  191 us (23%)
  local copies, waits for them, and re-layouts  148 us (18%)
  loops' own time  84.5 us (10%)
  starting transfers between devices  40.7 us (5%)
  waiting for transfers between devices  35.8 us (4%)
  matrix products  26.2 us (3%)
  between operations  19.7 us (2%)
    unnamed x2, blocking collectives  260 us
    select_n x63, other arithmetic, lap(): jnp.where(position < mine, new, old)  93.1 us
    add x63, other arithmetic, linked(): later[0] + (1.0 - later[1]) * earlier[0]  73.2 us
    another operation x1, loops' own time, prefix_2(): return lax.fori_loop(0, ahead, one, state)  43 us
    another operation x1, loops' own time, prefix(): return lax.fori_loop(0, count - 1, lap, so_far)  41.5 us
    dynamic_slice x63, local copies, waits for them, and re-layouts, lap(): longer = join(so_far, jax.tree.map(lambda part: part[position], pieces))  40.9 us
    dynamic_slice x63, local copies, waits for them, and re-layouts, one(): lax.dynamic_index_in_dim(a, source, 0, False).astype(own.dtype)  37.2 us
    unnamed x94, local copies, waits for them, and re-layouts  24.4 us
  transfers between devices with their start and end apart: 10, of which 5 were waited for; matrix products, arithmetic and copies ran while one was open for 26% of the time, Pallas kernels for 0%

profile of v1, /device:TPU:8, one launch (start us, length us, event | category | flops | bytes accessed | tf_op | source)
XLA Modules:
  0.0 805.5 jit_solution(13202837127730200551)
XLA Ops:
  9.5 5.6 all-to-all-start.1
  16.3 11.8 %all-to-all-done.1 = bf16[4,128,1024]{2,1,0:T(8,128)(2,1)S(1)} async-done(((bf16[4,128,1024]{2,1,0:T(8,128)(2,1)}), bf16[4,128,1024]{2,1,0:T(8,128)(2,1)S(1)}, u32[]{:S(2)}, u32[]{:S(2)}) %all-to-all-start.1) | async-done | bytes 1048608 | tf_op jit(solution)/shard_map/all_to_all | solution.py:68
  28.1 4.9 all-to-all-start.2
  37.5 7.6 all-to-all-done.2
  49.9 4.9 all-to-all-start
  57.4 8.4 %all-to-all-done = bf16[128,4,1024]{0,2,1:T(8,128)(2,1)S(1)} async-done(((bf16[128,4,1024]{0,2,1:T(8,128)(2,1)}), bf16[128,4,1024]{0,2,1:T(8,128)(2,1)S(1)}, u32[]{:S(2)}, u32[]{:S(2)}) %all-to-all-start) | async-done | bytes 1048608 | tf_op jit(solution)/shard_map/all_to_all | solution.py:66
  65.8 5.7 all-to-all-start.4
  76.8 134.0 %all-reduce.2 = f32[64]{0:T(128)S(1)} all-reduce(f32[64]{0:T(128)S(1)} %dynamic-update-slice.10), channel_id=1, replica_groups=mesh['seq'=64,'head'=4] {'seq'}, use_global_device_ids=true, to_apply=%add.2 | all-reduce | flops 64 | bytes 512
  213.1 2.7 fusion.23
  225.1 2.5 slice_convert_fusion.1
  232.3 2.5 copy.303
  235.0 2.6 bitcast_select_fusion
  244.5 175.6 %while.35 = (s32[]{:T(128)}, f32[8,128,128]{2,1,0:T(8,128)S(1)}, s32[]{:T(128)}, f32[64,8,128,128]{3,2,1,0:T(8,128)}, f32[64]{0:T(128)S(1)}, /*index=5*/s32[]{:T(128)}, f32[1]{0:T(128)}, s32[]{:T(128)}) while((s32[]{:T(128)}, f32[8,128,128]{2,1,0:T(8,128)S(1)}, s32[]{:T(128)}, f32[64,8,128,128]{3,2,1,0:T(8,128)}, f32[64]{0:T(128)S(1)}, ...), condition=%wide.region_4.5_spmd.clone, body=%wide.region_3.4_spmd.clone.sunk | while | flops 524293 | bytes 1573001 | solution.py:20
  431.3 2.5 copy.254
  437.3 2.6 copy.261
  439.9 2.9 pad_maximum_fusion
  442.8 2.9 copy.262
  445.7 3.0 copy.263
  448.7 3.1 fusion.7
  451.8 4.8 all-to-all-start.5
  460.0 125.6 %all-reduce.3 = bf16[64]{0:T(256)(128)(2,1)S(1)} all-reduce(bf16[64]{0:T(256)(128)(2,1)S(1)} %dynamic-update-slice.11), channel_id=1, replica_groups=mesh['seq'=64,'head'=4] {'seq'}, use_global_device_ids=true, to_apply=%add.3 | all-reduce | flops 64 | bytes 256
  585.6 3.4 copy.305
  589.1 3.0 copy.291
  596.1 2.5 convolution_bitcast_fusion.1
  600.5 4.8 all-to-all-start.3
  605.3 153.4 %while.34 = (s32[]{:T(128)}, f32[8,128,128]{2,1,0:T(8,128)S(1)}, s32[]{:T(128)}, bf16[64,8,128,128]{3,2,1,0:T(8,128)(2,1)}, bf16[64]{0:T(256)(128)(2,1)S(1)}, /*...) while((s32[]{:T(128)}, f32[8,128,128]{2,1,0:T(8,128)S(1)}, s32[]{:T(128)}, ...), condition=%wide.region_11.12_spmd, body=%wide.region_10.11_spmd.sunk | while | flops 393223 | bytes 1310893 | solution.py:43
  758.7 3.4 fusion.12
  764.2 2.4 copy.275
  766.6 4.9 all-to-all-start.7
  777.1 5.5 all-to-all-done.7
  782.6 4.9 all-to-all-start.6
  795.0 2.4 all-to-all-done.6
  (413 shorter events, 323.1 us)
Async XLA Ops:
  8.4 6.8 copy-start.32
  9.5 18.5 %all-to-all-start.1 = ((bf16[4,128,1024]{2,1,0:T(8,128)(2,1)}), bf16[4,128,1024]{2,1,0:T(8,128)(2,1)S(1)}, u32[]{:S(2)}, u32[]{:S(2)}) async-start(bf16[4,128,1024]{2,1,0:T(8,128)(2,1)} %pad_maximum_fusion.1), calls=%async_computation.1 | async-start | bytes 2097152 | tf_op jit(solution)/shard_map/all_to_all | solution.py:68
  15.2 17.9 %copy-start.36 = (s32[8]{0:T(128)S(1)}, s32[8]{0:T(128)}, u32[]{:S(2)}) copy-start(s32[8]{0:T(128)} %param.25) | copy-start | bytes 100
  28.1 17.0 %all-to-all-start.2 = ((bf16[128,4,1024]{2,0,1:T(8,128)(2,1)}), bf16[128,4,1024]{2,0,1:T(8,128)(2,1)S(1)}, u32[]{:S(2)}, u32[]{:S(2)}) async-start(bf16[128,4,1024]{2,0,1:T(8,128)(2,1)} %bitcast.158), calls=%async_computation.2 | async-start | bytes 2097152 | tf_op jit(solution)/shard_map/all_to_all | solution.py:71
  33.0 211.5 %all-gather.5.cloned.1.call-start = ((), (), s32[]{:S(2)}) async-start(), calls=%async_computation.8 | async-start | bytes 34078720 | tf_op jit(solution)/shard_map/all_gather | solution.py:11
  37.2 7.9 copy-start.14
  49.9 15.8 %all-to-all-start = ((bf16[128,4,1024]{0,2,1:T(8,128)(2,1)}), bf16[128,4,1024]{0,2,1:T(8,128)(2,1)S(1)}, u32[]{:S(2)}, u32[]{:S(2)}) async-start(bf16[128,4,1024]{0,2,1:T(8,128)(2,1)} %bitcast.189), calls=%async_computation | async-start | bytes 2097152 | tf_op jit(solution)/shard_map/all_to_all | solution.py:66
  54.9 20.6 %copy-start.37 = (u32[256]{0:T(256)S(1)}, u32[256]{0:T(256)}, u32[]{:S(2)}) copy-start(u32[256]{0:T(256)} %constant.223) | copy-start | bytes 3076
  65.8 6.4 copy-start.2
  65.8 159.3 %all-to-all-start.4 = ((bf16[128,4,1024]{2,0,1:T(8,128)(2,1)}), bf16[128,4,1024]{2,0,1:T(8,128)(2,1)}, u32[]{:S(2)}, u32[]{:S(2)}) async-start(bf16[128,4,1024]{2,0,1:T(8,128)(2,1)} %bitcast.186), calls=%async_computation.4 | async-start | bytes 2097152 | tf_op jit(solution)/shard_map/all_to_all | solution.py:72
  71.5 533.9 %all-gather.7.cloned.1.call-start = ((), (), s32[]{:S(2)}) async-start(), calls=%async_computation.9 | async-start | bytes 17039360 | tf_op jit(solution)/shard_map/all_gather | solution.py:28
  222.9 197.3 %copy-start.6 = (bf16[256,8,128]{0,2,1:T(8,128)(2,1)}, bf16[256,8,128]{0,2,1:T(8,128)(2,1)S(1)}, u32[]{:S(2)}) copy-start(bf16[256,8,128]{0,2,1:T(8,128)(2,1)S(1)} %reshape.298) | copy-start | bytes 1572868
  225.1 3.6 copy-start.30
  234.8 2.9 copy-start.21
  235.0 4.1 copy-start.27
  237.7 2.9 copy-start.15
  237.7 2.9 copy-start.34
  420.2 2.7 copy-start.16
  420.2 2.7 copy-start.24
  426.3 3.2 copy-start.20
  426.3 9.1 %copy-start.18 = (bf16[256,8,128]{2,0,1:T(8,128)(2,1)}, bf16[256,8,128]{2,0,1:T(8,128)(2,1)S(1)}, u32[]{:S(2)}) copy-start(bf16[256,8,128]{2,0,1:T(8,128)(2,1)S(1)} %get-tuple-element.306) | copy-start | bytes 1572868
  430.0 3.8 copy-start.35
  445.7 3.0 copy-start.3
  451.8 148.7 %all-to-all-start.5 = ((bf16[4,128,1024]{1,2,0:T(8,128)(2,1)}), bf16[4,128,1024]{1,2,0:T(8,128)(2,1)}, u32[]{:S(2)}, u32[]{:S(2)}) async-start(bf16[4,128,1024]{1,2,0:T(8,128)(2,1)} %fusion.7), calls=%async_computation.5 | async-start | bytes 2097152 | tf_op jit(solution)/shard_map/all_to_all | solution.py:210
  589.1 3.0 copy-start.28
  589.1 3.0 copy-start.29
  592.1 4.0 copy-start.1
  600.5 166.1 %all-to-all-start.3 = ((bf16[4,128,1024]{2,1,0:T(8,128)(2,1)}), bf16[4,128,1024]{2,1,0:T(8,128)(2,1)}, u32[]{:S(2)}, u32[]{:S(2)}) async-start(bf16[4,128,1024]{2,1,0:T(8,128)(2,1)} %all_to_all.97), calls=%async_computation.3 | async-start | bytes 2097152 | tf_op jit(solution)/shard_map/all_to_all | solution.py:143
  764.2 7.3 copy-start.7
  766.6 6.6 copy-start.17
  766.6 16.0 %all-to-all-start.7 = ((bf16[4,128,1024]{1,2,0:T(8,128)(2,1)}), bf16[4,128,1024]{1,2,0:T(8,128)(2,1)}, u32[]{:S(2)}, u32[]{:S(2)}) async-start(bf16[4,128,1024]{1,2,0:T(8,128)(2,1)} %copy.275), calls=%async_computation.7 | async-start | bytes 2097152 | tf_op jit(solution)/shard_map/all_to_all | solution.py:212
  782.6 14.8 %all-to-all-start.6 = ((bf16[4,128,1024]{1,2,0:T(8,128)(2,1)}), bf16[4,128,1024]{1,2,0:T(8,128)(2,1)S(1)}, u32[]{:S(2)}, u32[]{:S(2)}) async-start(bf16[4,128,1024]{1,2,0:T(8,128)(2,1)} %copy.270), calls=%async_computation.6 | async-start | bytes 2097152 | tf_op jit(solution)/shard_map/all_to_all | solution.py:211
  (16 other events, 28.9 us)
Sparse Core Ops, SparseCore 0:
  48.7 145.0 all-gather.4
  427.6 95.6 all-gather.6
